TPU v7x, 32 devices: a whole 2x2x4 slice. The times are simulated.
32 devices in a mesh: worker: 4 (over x, core), outer: 4 (over z), mp: 2 (over y).
Axes of the slice: x: 2, y: 2, z: 4, core: 2. Of those that a mesh axis runs over, the one named last changes fastest.
Arguments:
- grads: float32 [4, 4, 3584, 4096], P('worker', 'outer', None, 'mp'), as said below
- center: float32 [3584, 4096], P(('worker', 'outer'), 'mp'), may hold values from -6 to 6
- radius: float32 [1], replicated, may hold values from 1.5 to 3.5
Outputs:
- center_out: float32 [3584, 4096], P(('worker', 'outer'), 'mp')
Inputs may be any that keep to these rules, and one draw needn't show every extreme that they name: `grads`: finite values.
All inputs are finite; a program needn't handle non-finite values.
Results may differ from a plain program's by a relative error of at most 0.0001.
Values sent between devices are 32-bit elements; how exact they have to be, the bound alone decides.
No kernel may reach another device: no remote copies, remote signals or barrier semaphores. Data moves between devices by JAX's collectives and lax.ppermute only.
A program may use at most 192 MiB of HBM per device.

v0:
```python
import math
import jax
import jax.numpy as jnp
from jax import lax
from jax.sharding import PartitionSpec as P

D = 3584
ITERS = 2
KVW = 4096
epsilon = 1e-06


def on_device(grads, center, radius):
    worker_count = lax.axis_size("worker") * lax.axis_size("outer")
    radius_total = radius[0] * math.sqrt(D * KVW)
    own_rows = center
    mine = grads.reshape(1, grads.shape[2], grads.shape[3])
    gathered = lax.all_to_all(mine, ("worker", "outer"), split_axis=1, concat_axis=0, tiled=True)
    for iteration in range(ITERS):
        difference = gathered - own_rows[None]
        partial_value = jnp.sum(difference * difference, axis=(1, 2))
        norm_sq = lax.psum(partial_value, ("worker", "outer", "mp"))
        factor = jnp.minimum(1.0, radius_total * lax.rsqrt(norm_sq + epsilon))
        summed = jnp.sum(factor[:, None, None] * difference, axis=0)
        own_rows = own_rows + summed / worker_count
    return own_rows


def solution(mesh):
    in_specs = (P("worker", "outer", None, "mp"), P(("worker", "outer"), "mp"), P())
    out_specs = P(("worker", "outer"), "mp")
    return jax.shard_map(
        on_device, mesh=mesh, in_specs=in_specs, out_specs=out_specs, check_vma=False
    )
```

profile of v0, /device:TPU:0, one launch (start us, length us, event | category | flops | bytes accessed | tf_op | source)
XLA Modules:
  0.0 934.4 jit_solution(12065390304282626729)
XLA Ops:
  0.0 23.7 %reshape.36 = f32[1,3584,2048]{2,0,1:T(1,128)} reshape(f32[1,1,3584,2048]{3,2,1,0:T(8,128)} %param.3) | data formatting | bytes 58720256 | tf_op jit(solution)/shard_map/reshape | solution.py:17
  23.7 0.0 copy-start.1
  23.7 7.6 all-to-all-start
  31.9 0.0 copy-done.1
  31.9 10.4 %sub.34 = f32[16,224,2048]{2,1,0:T(8,128)} broadcast(f32[224,2048]{1,0:T(8,128)S(1)} %copy-done.1), dimensions={1,2} | broadcast | bytes 31195136 | tf_op jit(solution)/shard_map/sub | solution.py:20
  42.3 42.5 %sub.35 = f32[1,3584,2048]{2,0,1:T(1,128)} reshape(f32[16,224,2048]{2,1,0:T(8,128)} %sub.34) | data formatting | bytes 58720256 | tf_op jit(solution)/shard_map/sub | solution.py:20
  84.8 580.0 %all-to-all-done = f32[1,3584,2048]{2,0,1:T(1,128)} async-done(((f32[1,3584,2048]{2,0,1:T(1,128)}), f32[1,3584,2048]{2,0,1:T(1,128)}, u32[]{:S(2)}, u32[]{:S(2)}) %all-to-all-start) | async-done | bytes 29360160 | tf_op jit(solution)/shard_map/all_to_all | solution.py:18
  664.9 45.4 %multiply_reduce_fusion.3 = f32[3584]{0:T(1024)S(1)} fusion(f32[1,3584,2048]{2,0,1:T(1,128)} %all-to-all-done, f32[1,3584,2048]{2,0,1:T(1,128)} %sub.35), kind=kLoop, calls=%fused_computation.3 | loop fusion | flops 22016512 | bytes 58734592 | tf_op jit(solution)/shard_map/reduce_sum | solution.py:21
  710.3 0.1 reduce_sum.43
  710.4 0.1 reduce_sum.52
  710.5 37.4 %psum.14 = f32[16]{0:T(128)S(1)} all-reduce(f32[16]{0:T(128)S(1)} %reduce_sum.52), channel_id=1, replica_groups=mesh['worker'=4,'outer'=4,'mp'=2] {'worker','outer','mp'}, use_global_device_ids=true, to_apply=%region_2.0 | all-reduce | flops 16 | bytes 128 | tf_op jit(solution)/shard_map/psum | solution.py:22
  747.9 17.7 %copy.4 = f32[1,3584,2048]{2,1,0:T(8,128)S(1)} copy(f32[1,3584,2048]{2,0,1:T(1,128)} %all-to-all-done) | data formatting | bytes 58720256
  765.6 0.0 copy-start
  765.6 0.0 copy-start.2
  765.6 10.3 %copy-done = f32[1,3584,2048]{2,1,0:T(8,128)} copy-done((f32[1,3584,2048]{2,1,0:T(8,128)}, f32[1,3584,2048]{2,1,0:T(8,128)S(1)}, u32[]{:S(2)}) %copy-start) | copy-done | bytes 29360152
  775.9 4.4 multiply_reduce_fusion.2
  780.3 0.0 copy-done.2
  780.3 0.3 multiply_add_fusion.1
  780.6 10.4 %sub.38 = f32[16,224,2048]{2,1,0:T(8,128)} broadcast(f32[224,2048]{1,0:T(8,128)S(1)} %multiply_add_fusion.1), dimensions={1,2} | broadcast | bytes 31195136 | tf_op jit(solution)/shard_map/sub | solution.py:20
  791.0 42.5 %sub.39 = f32[1,3584,2048]{2,0,1:T(1,128)} reshape(f32[16,224,2048]{2,1,0:T(8,128)} %sub.38) | data formatting | bytes 58720256 | tf_op jit(solution)/shard_map/sub | solution.py:20
  833.6 45.4 %multiply_reduce_fusion.1 = f32[3584]{0:T(1024)S(1)} fusion(f32[1,3584,2048]{2,0,1:T(1,128)} %all-to-all-done, f32[1,3584,2048]{2,0,1:T(1,128)} %sub.39), kind=kLoop, calls=%fused_computation.1 | loop fusion | flops 22016512 | bytes 58734592 | tf_op jit(solution)/shard_map/reduce_sum | solution.py:21
  879.0 0.1 reduce_sum.55
  879.0 0.1 reduce_sum.56
  879.2 41.8 %psum.15 = f32[16]{0:T(128)S(1)} all-reduce(f32[16]{0:T(128)S(1)} %reduce_sum.56), channel_id=1, replica_groups=mesh['worker'=4,'outer'=4,'mp'=2] {'worker','outer','mp'}, use_global_device_ids=true, to_apply=%region_6.7 | all-reduce | flops 16 | bytes 128 | tf_op jit(solution)/shard_map/psum | solution.py:22
  920.9 11.9 %multiply_reduce_fusion = f32[224,2048]{1,0:T(8,128)S(1)} fusion(f32[16,224,2048]{2,1,0:T(8,128)} %bitcast.5, f32[16]{0:T(128)S(1)} %multiply_minimum_fusion, f32[224,2048]{1,0:T(8,128)S(1)} %multiply_add_fusion.1), kind=kLoop, calls=%fused_computation | loop fusion | flops 21561344 | bytes 33030208 | tf_op jit(solution)/shard_map/reduce_sum | solution.py:24
  932.8 1.5 multiply_add_fusion
  (2 shorter events, 0.0 us)
Async XLA Ops:
  23.7 8.2 copy-start.1
  23.7 641.2 %all-to-all-start = ((f32[1,3584,2048]{2,0,1:T(1,128)}), f32[1,3584,2048]{2,0,1:T(1,128)}, u32[]{:S(2)}, u32[]{:S(2)}) async-start(f32[1,3584,2048]{2,0,1:T(1,128)} %reshape.36), calls=%async_computation | async-start | bytes 58720256 | tf_op jit(solution)/shard_map/all_to_all | solution.py:18
  765.6 10.3 %copy-start = (f32[1,3584,2048]{2,1,0:T(8,128)}, f32[1,3584,2048]{2,1,0:T(8,128)S(1)}, u32[]{:S(2)}) copy-start(f32[1,3584,2048]{2,1,0:T(8,128)S(1)} %copy.4) | copy-start | bytes 88080384
  765.6 14.7 %copy-start.2 = (f32[224,2048]{1,0:T(8,128)S(1)}, f32[224,2048]{1,0:T(8,128)}, u32[]{:S(2)}) copy-start(f32[224,2048]{1,0:T(8,128)} %param.4) | copy-start | bytes 5505028
where the time goes:
time: 937 us; the launch traced here: 934 us
  waiting for transfers between devices  580 us (62%)
  local copies, waits for them, and re-layouts  158 us (17%)
  other arithmetic  109 us (12%)
  blocking collectives  79.2 us (8%)
    all_to_all x1, waiting for transfers between devices, on_device(): lax.all_to_all(mine, ('worker', 'outer'), split_axis=1, concat_axis=0, ti...  580 us
    sub x4, local copies, waits for them, and re-layouts, on_device(): difference = gathered - own_rows[None]  106 us
    reduce_sum x4, other arithmetic, on_device(): partial_value = jnp.sum(difference * difference, axis=(1, 2))  91.1 us
    psum x2, blocking collectives, on_device(): norm_sq = lax.psum(partial_value, ('worker', 'outer', 'mp'))  79.2 us
    unnamed x7, local copies, waits for them, and re-layouts  28 us
    reshape x1, local copies, waits for them, and re-layouts, on_device(): mine = grads.reshape(1, grads.shape[2], grads.shape[3])  23.7 us
  transfers between devices with their start and end apart: 1, of which 1 were waited for; matrix products, arithmetic and copies ran while one was open for 6% of the time, Pallas kernels for 0%

commit v1 on v0

--- a/solution.py
+++ b/solution.py
@@ -10,12 +10,24 @@
 epsilon = 1e-06
 
 
+def scan_the_yards(local):
+    return jnp.concatenate(
+        jax.lax.all_to_all(
+            jnp.stack(jnp.split(local, jax.lax.psum(1, ("worker", "outer")), axis=1), axis=0),
+            ("worker", "outer"),
+            split_axis=0,
+            concat_axis=0,
+        ),
+        axis=0,
+    )
+
+
 def on_device(grads, center, radius):
     worker_count = lax.axis_size("worker") * lax.axis_size("outer")
     radius_total = radius[0] * math.sqrt(D * KVW)
     own_rows = center
     mine = grads.reshape(1, grads.shape[2], grads.shape[3])
-    gathered = lax.all_to_all(mine, ("worker", "outer"), split_axis=1, concat_axis=0, tiled=True)
+    gathered = scan_the_yards(mine)
     for iteration in range(ITERS):
         difference = gathered - own_rows[None]
         partial_value = jnp.sum(difference * difference, axis=(1, 2))

time: 937 us -> 807 us (0.86)
  local copies, waits for them, and re-layouts: 158 us -> 37.5 us
  other arithmetic: 109 us -> 48.9 us
  waiting for transfers between devices: 580 us -> 633 us
    sub x4 -> x0, local copies, waits for them, and re-layouts: 106 us -> none  [on_device(): difference = gathered - own_rows[None]]
    reduce_sum x4 -> x2, other arithmetic: 91.1 us -> 23.2 us  [on_device(): partial_value = jnp.sum(difference * difference, axis=(1, 2))]
    all_to_all x1, waiting for transfers between devices: 580 us -> 633 us  [scan_the_yards(): jax.lax.all_to_all(jnp.stack(jnp.split(local, jax.lax.psum(1, ('worker',...]
    reshape x1 -> x0, local copies, waits for them, and re-layouts: 23.7 us -> none  [on_device(): mine = grads.reshape(1, grads.shape[2], grads.shape[3])]
    unnamed x7 -> x21, local copies, waits for them, and re-layouts: 28 us -> 36.1 us
  transfers between devices with their start and end apart: 1 -> 1, of which waited for: 1 -> 1; matrix products, arithmetic and copies ran while one was open for 6% -> 0% of each run, Pallas kernels for 0% -> 0%
where the time goes in v1:
time: 807 us
  waiting for transfers between devices  633 us (78%)
  blocking collectives  79.1 us (10%)
  other arithmetic  48.9 us (6%)
  local copies, waits for them, and re-layouts  37.5 us (5%)
    all_to_all x1, waiting for transfers between devices, scan_the_yards(): jax.lax.all_to_all(jnp.stack(jnp.split(local, jax.lax.psum(1, ('worker',...  633 us
    psum x2, blocking collectives, on_device(): norm_sq = lax.psum(partial_value, ('worker', 'outer', 'mp'))  79.1 us
    unnamed x21, local copies, waits for them, and re-layouts  36.1 us
    reduce_sum x2, other arithmetic, on_device(): summed = jnp.sum(factor[:, None, None] * difference, axis=0)  23.9 us
    reduce_sum x2, other arithmetic, on_device(): partial_value = jnp.sum(difference * difference, axis=(1, 2))  23.2 us
  transfers between devices with their start and end apart: 1, of which 1 were waited for; matrix products, arithmetic and copies ran while one was open for 0% of the time, Pallas kernels for 0%

profile of v1, /device:TPU:0, one launch (start us, length us, event | category | flops | bytes accessed | tf_op | source)
XLA Modules:
  0.0 806.7 jit_solution(8485957217396782042)
XLA Ops:
  0.0 0.0 copy-start
  0.0 3.1 fusion.15
  3.1 3.7 fusion.14
  6.8 3.7 fusion.13
  10.5 3.7 fusion.12
  14.2 3.0 fusion.11
  17.2 2.9 fusion.10
  20.1 3.0 fusion.9
  23.0 3.0 fusion.8
  26.0 0.0 copy-done
  26.0 1.4 fusion.7
  27.4 1.5 fusion.6
  28.9 1.4 fusion.5
  30.3 1.4 fusion.4
  31.7 1.4 fusion.3
  33.2 1.5 fusion.2
  34.6 1.4 fusion.1
  36.1 1.4 fusion
  37.5 0.0 copy-start.1
  37.5 7.6 all-to-all-start
  45.7 633.0 %all-to-all-done = f32[16,1,224,2048]{3,2,1,0:T(8,128)} async-done(((f32[16,1,224,2048]{3,2,1,0:T(8,128)}), f32[16,1,224,2048]{3,2,1,0:T(8,128)}, u32[]{:S(2)}, u32[]{:S(2)}) %all-to-all-start) | async-done | bytes 29360160 | tf_op jit(solution)/shard_map/all_to_all | solution.py:15
  678.7 0.0 copy-done.1
  678.7 11.6 %multiply_reduce_fusion.3 = f32[16]{0:T(128)S(1)} fusion(f32[16,1,224,2048]{3,2,1,0:T(8,128)} %all-to-all-done, f32[224,2048]{1,0:T(8,128)S(1)} %copy-done.1), kind=kLoop, calls=%fused_computation.5 | loop fusion | flops 22020080 | bytes 31195200 | tf_op jit(solution)/shard_map/reduce_sum | solution.py:33
  690.3 37.4 %psum.14 = f32[16]{0:T(128)S(1)} all-reduce(f32[16]{0:T(128)S(1)} %multiply_reduce_fusion.3), channel_id=1, replica_groups=mesh['worker'=4,'outer'=4,'mp'=2] {'worker','outer','mp'}, use_global_device_ids=true, to_apply=%region_1.0 | all-reduce | flops 16 | bytes 128 | tf_op jit(solution)/shard_map/psum | solution.py:34
  727.7 0.0 copy-start.2
  727.7 12.0 %multiply_reduce_fusion.2 = f32[224,2048]{1,0:T(8,128)S(1)} fusion(f32[16,1,224,2048]{3,2,1,0:T(8,128)} %all-to-all-done, f32[16]{0:T(128)S(1)} %multiply_minimum_fusion.1, f32[224,2048]{1,0:T(8,128)S(1)} %copy-done.1), kind=kLoop, calls=%fused_computation.4 | loop fusion | flops 21561344 | bytes 33030208 | tf_op jit(solution)/shard_map/reduce_sum | solution.py:36
  739.7 0.0 copy-done.2
  739.7 0.2 multiply_add_fusion.1
  739.9 11.6 %multiply_reduce_fusion.1 = f32[16]{0:T(128)S(1)} fusion(f32[16,1,224,2048]{3,2,1,0:T(8,128)} %all-to-all-done, f32[224,2048]{1,0:T(8,128)S(1)} %multiply_add_fusion.1), kind=kLoop, calls=%fused_computation.3 | loop fusion | flops 22020080 | bytes 31195200 | tf_op jit(solution)/shard_map/reduce_sum | solution.py:33
  751.5 41.7 %psum.15 = f32[16]{0:T(128)S(1)} all-reduce(f32[16]{0:T(128)S(1)} %multiply_reduce_fusion.1), channel_id=1, replica_groups=mesh['worker'=4,'outer'=4,'mp'=2] {'worker','outer','mp'}, use_global_device_ids=true, to_apply=%region_4.0 | all-reduce | flops 16 | bytes 128 | tf_op jit(solution)/shard_map/psum | solution.py:34
  793.3 11.9 %multiply_reduce_fusion = f32[224,2048]{1,0:T(8,128)S(1)} fusion(f32[16,1,224,2048]{3,2,1,0:T(8,128)} %all-to-all-done, f32[16]{0:T(128)S(1)} %multiply_minimum_fusion, f32[224,2048]{1,0:T(8,128)S(1)} %multiply_add_fusion.1), kind=kLoop, calls=%fused_computation.2 | loop fusion | flops 21561344 | bytes 33030208 | tf_op jit(solution)/shard_map/reduce_sum | solution.py:36
  805.2 1.5 multiply_add_fusion
  (2 shorter events, 0.0 us)
Async XLA Ops:
  0.0 26.0 %copy-start = (f32[1,1,3584,2048]{3,2,1,0:T(8,128)S(1)}, f32[1,1,3584,2048]{3,2,1,0:T(8,128)}, u32[]{:S(2)}) copy-start(f32[1,1,3584,2048]{3,2,1,0:T(8,128)} %param.3) | copy-start | bytes 88080384
  37.5 641.2 %copy-start.1 = (f32[224,2048]{1,0:T(8,128)S(1)}, f32[224,2048]{1,0:T(8,128)}, u32[]{:S(2)}) copy-start(f32[224,2048]{1,0:T(8,128)} %param.4) | copy-start | bytes 5505028
  37.5 641.2 %all-to-all-start = ((f32[16,1,224,2048]{3,2,1,0:T(8,128)}), f32[16,1,224,2048]{3,2,1,0:T(8,128)}, u32[]{:S(2)}, u32[]{:S(2)}) async-start(f32[16,1,224,2048]{3,2,1,0:T(8,128)} %fusion), calls=%async_computation | async-start | bytes 58720256 | tf_op jit(solution)/shard_map/all_to_all | solution.py:15
  727.7 12.0 %copy-start.2 = (f32[224,2048]{1,0:T(8,128)S(1)}, f32[224,2048]{1,0:T(8,128)}, u32[]{:S(2)}) copy-start(f32[224,2048]{1,0:T(8,128)} %param.4) | copy-start | bytes 5505028

commit v2 on v0

--- a/solution.py
+++ b/solution.py
@@ -19,7 +19,9 @@
     for iteration in range(ITERS):
         difference = gathered - own_rows[None]
         partial_value = jnp.sum(difference * difference, axis=(1, 2))
-        norm_sq = lax.psum(partial_value, ("worker", "outer", "mp"))
+        norm_sq = partial_value
+        for no in ("worker", ("outer", "mp")):
+            norm_sq = lax.psum(norm_sq, axis_name=no)
         factor = jnp.minimum(1.0, radius_total * lax.rsqrt(norm_sq + epsilon))
         summed = jnp.sum(factor[:, None, None] * difference, axis=0)
         own_rows = own_rows + summed / worker_count

time: 937 us -> 907 us (0.968)
  blocking collectives: 79.2 us -> 48.9 us
    psum x2 -> x4, blocking collectives: 79.2 us -> 48.9 us  [on_device(): norm_sq = lax.psum(norm_sq, axis_name=no)]
where the time goes in v2:
time: 907 us; the launch traced here: 904 us
  waiting for transfers between devices  580 us (64%)
  local copies, waits for them, and re-layouts  158 us (17%)
  other arithmetic  109 us (12%)
  blocking collectives  48.9 us (5%)
    all_to_all x1, waiting for transfers between devices, on_device(): lax.all_to_all(mine, ('worker', 'outer'), split_axis=1, concat_axis=0, ti...  580 us
    sub x4, local copies, waits for them, and re-layouts, on_device(): difference = gathered - own_rows[None]  106 us
    reduce_sum x4, other arithmetic, on_device(): partial_value = jnp.sum(difference * difference, axis=(1, 2))  91.1 us
    psum x4, blocking collectives, on_device(): norm_sq = lax.psum(norm_sq, axis_name=no)  48.9 us
    unnamed x7, local copies, waits for them, and re-layouts  28 us
    reshape x1, local copies, waits for them, and re-layouts, on_device(): mine = grads.reshape(1, grads.shape[2], grads.shape[3])  23.7 us
  transfers between devices with their start and end apart: 1, of which 1 were waited for; matrix products, arithmetic and copies ran while one was open for 6% of the time, Pallas kernels for 0%

profile of v2, /device:TPU:0, one launch (start us, length us, event | category | flops | bytes accessed | tf_op | source)
XLA Modules:
  0.0 904.1 jit_solution(15798235343436848863)
XLA Ops:
  0.0 23.7 %reshape.36 = f32[1,3584,2048]{2,0,1:T(1,128)} reshape(f32[1,1,3584,2048]{3,2,1,0:T(8,128)} %param.3) | data formatting | bytes 58720256 | tf_op jit(solution)/shard_map/reshape | solution.py:17
  23.7 0.0 copy-start.1
  23.7 7.6 all-to-all-start
  31.9 0.0 copy-done.1
  31.9 10.4 %sub.34 = f32[16,224,2048]{2,1,0:T(8,128)} broadcast(f32[224,2048]{1,0:T(8,128)S(1)} %copy-done.1), dimensions={1,2} | broadcast | bytes 31195136 | tf_op jit(solution)/shard_map/sub | solution.py:20
  42.3 42.5 %sub.35 = f32[1,3584,2048]{2,0,1:T(1,128)} reshape(f32[16,224,2048]{2,1,0:T(8,128)} %sub.34) | data formatting | bytes 58720256 | tf_op jit(solution)/shard_map/sub | solution.py:20
  84.8 580.0 %all-to-all-done = f32[1,3584,2048]{2,0,1:T(1,128)} async-done(((f32[1,3584,2048]{2,0,1:T(1,128)}), f32[1,3584,2048]{2,0,1:T(1,128)}, u32[]{:S(2)}, u32[]{:S(2)}) %all-to-all-start) | async-done | bytes 29360160 | tf_op jit(solution)/shard_map/all_to_all | solution.py:18
  664.9 45.4 %multiply_reduce_fusion.3 = f32[3584]{0:T(1024)S(1)} fusion(f32[1,3584,2048]{2,0,1:T(1,128)} %all-to-all-done, f32[1,3584,2048]{2,0,1:T(1,128)} %sub.35), kind=kLoop, calls=%fused_computation.3 | loop fusion | flops 22016512 | bytes 58734592 | tf_op jit(solution)/shard_map/reduce_sum | solution.py:21
  710.3 0.1 reduce_sum.43
  710.4 0.1 reduce_sum.52
  710.5 6.2 psum.28
  716.7 19.8 %psum.29 = f32[16]{0:T(128)S(1)} all-reduce(f32[16]{0:T(128)S(1)} %psum.28), channel_id=1, replica_groups=mesh['worker'=4,'outer'=4,'mp'=2] {'outer','mp'}, use_global_device_ids=true, to_apply=%region_3.0 | all-reduce | flops 16 | bytes 128 | tf_op jit(solution)/shard_map/psum | solution.py:24
  736.5 17.7 %copy.4 = f32[1,3584,2048]{2,1,0:T(8,128)S(1)} copy(f32[1,3584,2048]{2,0,1:T(1,128)} %all-to-all-done) | data formatting | bytes 58720256
  754.2 0.0 copy-start
  754.2 0.0 copy-start.2
  754.2 10.3 %copy-done = f32[1,3584,2048]{2,1,0:T(8,128)} copy-done((f32[1,3584,2048]{2,1,0:T(8,128)}, f32[1,3584,2048]{2,1,0:T(8,128)S(1)}, u32[]{:S(2)}) %copy-start) | copy-done | bytes 29360152
  764.6 4.4 multiply_reduce_fusion.2
  768.9 0.0 copy-done.2
  768.9 0.3 multiply_add_fusion.1
  769.3 10.4 %sub.38 = f32[16,224,2048]{2,1,0:T(8,128)} broadcast(f32[224,2048]{1,0:T(8,128)S(1)} %multiply_add_fusion.1), dimensions={1,2} | broadcast | bytes 31195136 | tf_op jit(solution)/shard_map/sub | solution.py:20
  779.6 42.5 %sub.39 = f32[1,3584,2048]{2,0,1:T(1,128)} reshape(f32[16,224,2048]{2,1,0:T(8,128)} %sub.38) | data formatting | bytes 58720256 | tf_op jit(solution)/shard_map/sub | solution.py:20
  822.2 45.4 %multiply_reduce_fusion.1 = f32[3584]{0:T(1024)S(1)} fusion(f32[1,3584,2048]{2,0,1:T(1,128)} %all-to-all-done, f32[1,3584,2048]{2,0,1:T(1,128)} %sub.39), kind=kLoop, calls=%fused_computation.1 | loop fusion | flops 22016512 | bytes 58734592 | tf_op jit(solution)/shard_map/reduce_sum | solution.py:21
  867.6 0.1 reduce_sum.55
  867.7 0.1 reduce_sum.56
  867.8 5.8 psum.30
  873.6 17.1 %psum.31 = f32[16]{0:T(128)S(1)} all-reduce(f32[16]{0:T(128)S(1)} %psum.30), channel_id=1, replica_groups=mesh['worker'=4,'outer'=4,'mp'=2] {'outer','mp'}, use_global_device_ids=true, to_apply=%region_8.9 | all-reduce | flops 16 | bytes 128 | tf_op jit(solution)/shard_map/psum | solution.py:24
  890.7 11.9 %multiply_reduce_fusion = f32[224,2048]{1,0:T(8,128)S(1)} fusion(f32[16,224,2048]{2,1,0:T(8,128)} %bitcast.5, f32[16]{0:T(128)S(1)} %multiply_minimum_fusion, f32[224,2048]{1,0:T(8,128)S(1)} %multiply_add_fusion.1), kind=kLoop, calls=%fused_computation | loop fusion | flops 21561344 | bytes 33030208 | tf_op jit(solution)/shard_map/reduce_sum | solution.py:26
  902.6 1.5 multiply_add_fusion
  (2 shorter events, 0.0 us)
Async XLA Ops:
  23.7 8.2 copy-start.1
  23.7 641.2 %all-to-all-start = ((f32[1,3584,2048]{2,0,1:T(1,128)}), f32[1,3584,2048]{2,0,1:T(1,128)}, u32[]{:S(2)}, u32[]{:S(2)}) async-start(f32[1,3584,2048]{2,0,1:T(1,128)} %reshape.36), calls=%async_computation | async-start | bytes 58720256 | tf_op jit(solution)/shard_map/all_to_all | solution.py:18
  754.2 10.3 %copy-start = (f32[1,3584,2048]{2,1,0:T(8,128)}, f32[1,3584,2048]{2,1,0:T(8,128)S(1)}, u32[]{:S(2)}) copy-start(f32[1,3584,2048]{2,1,0:T(8,128)S(1)} %copy.4) | copy-start | bytes 88080384
  754.2 14.7 %copy-start.2 = (f32[224,2048]{1,0:T(8,128)S(1)}, f32[224,2048]{1,0:T(8,128)}, u32[]{:S(2)}) copy-start(f32[224,2048]{1,0:T(8,128)} %param.4) | copy-start | bytes 5505028
